TPU v7x, 32 devices: a whole 2x2x4 slice. The times are simulated.
32 devices in a mesh: seq: 16 (over z, x, core), tp: 2 (over y).
Axes of the slice: x: 2, y: 2, z: 4, core: 2. Of those that a mesh axis runs over, the one named last changes fastest.
Arguments:
- tokens: bfloat16 [8192, 4096], P('seq'), may hold values from -6 to 6
- w_in: bfloat16 [4096, 3, 4096], P('seq', None, 'tp'), may hold values from -0.09375 to 0.09375
- short_taps: float32 [3, 3, 4096], P(None, None, 'tp'), may hold values from -3 to 3
- decay_rate: float32 [256, 16], P('tp'), may hold values from 1.2207031e-05 to 0.04, as said below
- residue: float32 [256, 16], P('tp'), may hold values from -4 to 4
- skip_gain: float32 [4096], P('tp'), may hold values from -4 to 4
- w_out: bfloat16 [4096, 4096], P('tp'), may hold values from -0.125 to 0.125
Outputs:
- mixed: bfloat16 [8192, 4096], P('seq', 'tp')
Inputs may be any that keep to these rules, and one draw needn't show every extreme that they name: `decay_rate`: every decay rate is positive.
All inputs are finite; a program needn't handle non-finite values.
Results may differ from a plain program's by a relative error of at most 0.0075.
Values may be sent and summed in bfloat16 or wider, within the bound.
A program may use at most 192 MiB of HBM per device.

v0:
```python
import jax
import jax.numpy as jnp
from jax import lax
from jax.sharding import PartitionSpec as P

SUB = 128


def passed_along(block, axis, distance):
    devices = range(lax.axis_size(axis))
    route = [(i - distance, i) for i in devices if i - distance in devices]
    return lax.ppermute(block, axis, route)


def prefix(value, axis, combine, identity):
    peers, here = (lax.axis_size(axis), lax.axis_index(axis))
    everything = jax.tree.map(lambda part: lax.all_gather(part, axis), value)
    start = jax.tree.map(
        lambda part, zero: jnp.broadcast_to(jnp.asarray(zero, part.dtype), part.shape),
        value,
        identity,
    )

    def step(k, before):
        reached = k < here
        new = combine(before, jax.tree.map(lambda part: part[k], everything))
        return jax.tree.map(lambda a, b: jnp.where(reached, a, b), new, before)

    return lax.fori_loop(0, peers, step, start)


def shards(tokens, w_in, short_taps, decay_rate, residue, skip_gain, w_out):
    count = tokens.shape[0]
    chans = w_in.shape[2]
    groups = decay_rate.shape[0]
    order = decay_rate.shape[1]
    width = chans // groups
    taps = short_taps.shape[0]
    highest = lax.Precision.HIGHEST
    piece = lax.all_gather(w_in, "seq", axis=0, tiled=True)
    summed = jnp.dot(
        tokens, piece.reshape(piece.shape[0], 3 * chans), preferred_element_type=jnp.float32
    )
    proj = summed.astype(jnp.bfloat16).reshape(count, 3, chans)
    before = passed_along(proj[count - (taps - 1) :], "seq", 1)
    padded = jnp.concatenate([before, proj], axis=0).astype(jnp.float32)
    filtered = jnp.zeros((count, 3, chans), jnp.float32)
    for tap in range(taps):
        filtered = filtered + short_taps[tap] * padded[taps - 1 - tap : taps - 1 - tap + count]
    query = filtered[:, 0]
    gated = filtered[:, 1] * filtered[:, 2]
    weight_mode = residue * jnp.sqrt(2.0 * decay_rate / order)
    offsets = jnp.arange(SUB, dtype=jnp.float32)
    kernel = jnp.einsum(
        "gm,gmd->gd",
        weight_mode,
        jnp.exp(-decay_rate[:, :, None] * offsets[None, None, :]),
        precision=highest,
    )
    lag = jnp.arange(SUB)[:, None] - jnp.arange(SUB)[None, :]
    toeplitz = jnp.where(lag[None] >= 0, kernel[:, jnp.maximum(lag, 0)], 0.0)
    enter = weight_mode[:, None, :] * jnp.exp(
        -decay_rate[:, None, :] * (offsets[None, :, None] + 1.0)
    )
    leave = jnp.exp(-decay_rate[:, :, None] * (SUB - 1.0 - offsets[None, None, :]))
    fade = jnp.exp(-decay_rate * SUB)[:, :, None]
    blocks = gated.reshape(count // SUB, SUB, groups, width)

    def advance(state, block):
        local = jnp.einsum("gij,jgc->igc", toeplitz, block, precision=highest)
        local = local + jnp.einsum("gim,gmc->igc", enter, state, precision=highest)
        state = fade * state + jnp.einsum("gmj,jgc->gmc", leave, block, precision=highest)
        return (state, local)

    final_state, local_out = lax.scan(
        advance, jnp.zeros((groups, order, width), jnp.float32), blocks
    )
    local_out = local_out.reshape(count, groups, width)

    def combine(earlier, later):
        return (earlier[0] * later[0], later[1] + later[0][:, :, None] * earlier[1])

    hop = jnp.exp(-decay_rate * count)
    _, entering = prefix(
        (hop, final_state), "seq", combine, (jnp.ones_like(hop), jnp.zeros_like(final_state))
    )
    positions = jnp.arange(count, dtype=jnp.float32)
    reach = weight_mode[:, None, :] * jnp.exp(
        -decay_rate[:, None, :] * (positions[None, :, None] + 1.0)
    )
    carried = jnp.einsum("gtm,gmc->tgc", reach, entering, precision=highest)
    conv = (local_out + carried).reshape(count, chans)
    mix = (query * (conv + skip_gain * gated)).astype(jnp.bfloat16)
    partial_value = jnp.dot(mix, w_out, preferred_element_type=jnp.float32)
    return lax.psum_scatter(
        partial_value.astype(jnp.bfloat16), "tp", scatter_dimension=1, tiled=True
    )


def solution(mesh):
    in_specs = (
        P("seq", None),
        P("seq", None, "tp"),
        P(None, None, "tp"),
        P("tp", None),
        P("tp", None),
        P("tp"),
        P("tp", None),
    )
    out_specs = P("seq", "tp")
    return jax.shard_map(shards, mesh=mesh, in_specs=in_specs, out_specs=out_specs, check_vma=False)
```

profile of v0, /device:TPU:0, one launch (start us, length us, event | category | flops | bytes accessed | tf_op | source)
XLA Modules:
  0.0 692.5 jit_solution(16612572888679851134)
XLA Ops:
  6.5 4.8 copy.46
  11.7 0.6 multiply_reduce_fusion
  12.4 54.7 %gather_fusion = f32[16384,128]{1,0:T(8,128)} fusion(f32[128,128]{0,1:T(8,128)S(1)} %copy.62, s32[16384]{0:T(1024)S(1)} %bitcast_clamp_fusion), kind=kCustom, calls=%fused_computation | custom fusion | bytes 16842752 | tf_op jit(solution)/shard_map/gather | solution.py:61
  67.2 9.4 %copy.50 = f32[128,128,128]{1,0,2:T(8,128)} copy(f32[128,128,128]{2,1,0:T(8,128)} %bitcast.89) | data formatting | bytes 16777216 | tf_op jit(solution)/shard_map/gather | solution.py:61
  76.6 8.3 %select_bitcast_fusion = f32[128,128,128]{2,1,0:T(8,128)} fusion(f32[128,128,128]{1,0,2:T(8,128)} %copy.50, pred[128,128]{1,0:T(8,128)(4,1)S(1)} %subtract_compare_fusion), kind=kLoop, calls=%fused_computation.30 | loop fusion | flops 2097152 | bytes 16793600 | tf_op jit(solution)/shard_map/jit(_where)/select_n | solution.py:61
  84.9 185.2 %all-gather.5.cloned.1.call-done = bf16[4096,3,2048]{0,2,1:T(8,128)(2,1)} async-done(((bf16[256,3,2048]{0,2,1:T(8,128)(2,1)}), bf16[4096,3,2048]{0,2,1:T(8,128)(2,1)}) %all-gather.5.cloned.1.call-update) | async-done | bytes 50331664 | tf_op jit(solution)/shard_map/all_gather | solution.py:40
  270.1 33.7 %convolution_convert_fusion = bf16[512,6144]{1,0:T(8,128)(2,1)} fusion(bf16[512,4096]{1,0:T(8,128)(2,1)} %param.11, bf16[4096,6144]{0,1:T(8,128)(2,1)} %bitcast.96), kind=kOutput, calls=%fused_computation.29 | convolution fusion | flops 25772949504 | bytes 60817408 | tf_op jit(solution)/shard_map/dot_general | solution.py:41
  303.8 0.9 slice.46
  304.8 2.3 collective-permute-start
  307.2 8.7 %copy.47 = bf16[512,6144]{0,1:T(8,128)(2,1)} copy(bf16[512,6144]{1,0:T(8,128)(2,1)} %convolution_convert_fusion) | data formatting | bytes 12582912 | tf_op jit(solution)/shard_map/convert_element_type | solution.py:44
  315.8 0.9 copy.48
  316.7 11.7 %maximum_convert_fusion = f32[514,3,2048]{0,2,1:T(8,128)} fusion(bf16[512,3,2048]{0,2,1:T(8,128)(2,1)} %bitcast.90, bf16[2,3,2048]{0,2,1:T(8,128)(2,1)S(1)} %copy.48), kind=kLoop, calls=%fused_computation.31 | loop fusion | flops 12632064 | bytes 18948096 | tf_op jit(solution)/shard_map/convert_element_type | solution.py:46
  328.4 17.5 %fusion.19 = f32[512,3,2048]{0,2,1:T(8,128)S(1)} fusion(f32[514,3,2048]{0,2,1:T(8,128)} %maximum_convert_fusion, f32[3,2048]{1,0:T(4,128)S(1)} %get-tuple-element.340, f32[3,2048]{1,0:T(4,128)S(1)} %get-tuple-element.341, f32[3,2048]{1,0:T(4,128)S(1)} %get-tuple-element.339), kind=kLoop, calls=%fused_computation.25 | loop fusion | flops 15728640 | bytes 50405376 | tf_op jit(solution)/shard_map/add | solution.py:49
  345.9 4.5 copy-done
  350.4 3.0 slice_multiply_fusion.3
  353.4 5.2 mul.180
  358.6 198.3 %while.30 = (s32[]{:T(128)}, f32[128,16,16]{1,2,0:T(8,128)S(1)}, f32[4,128,128,16]{1,0,3,2:T(4,128)}, f32[128,16,1]{1,0,2:T(8,128)S(1)}, f32[4,128,128,16]{1,0,3...) while((s32[]{:T(128)}, f32[128,16,16]{1,2,0:T(8,128)S(1)}, ...), condition=%wide.region_1.2_spmd.clone.clone.clone, body=%wide.region_0.1_spmd.clone.clone.clone.sunk | while | flops 504496128 | bytes 18252936 | solution.py:75
  358.6 3.3 constant_dynamic-slice_fusion.5
  362.0 15.4 %fusion.57 = f32[128,16,128]{2,1,0:T(8,128)S(1)} fusion(f32[128,128,16]{0,2,1:T(8,128)S(1)} %bitcast.86, f32[128,128,128]{2,1,0:T(8,128)} %get-tuple-element.468), kind=kOutput, calls=%fused_computation.59.clone.1 | convolution fusion | flops 402653184 | bytes 10485760 | tf_op jit(solution)/shard_map/while/body/eval_jaxpr/gij,jgc->igc/dot_general | solution.py:70
  377.3 2.4 convolution_add_fusion.2
  379.7 26.6 %dynamic_update_slice.8 = f32[4,128,128,16]{1,0,3,2:T(4,128)} dynamic-update-slice(f32[4,128,128,16]{1,0,3,2:T(4,128)} %get-tuple-element.453, f32[1,128,128,16]{1,0,3,2:T(1,128)} %bitcast.88, s32[]{:T(128)} %get-tuple-element.451, s32[]{:T(128)} %constant.52.clone.1..sunk.1, s32[]{:T(128)} %constant.52.clone.1..sunk.1, s32[]{:T(128)} %constant.52.clone.1..sunk.1) | dynamic-update-slice | bytes 2097156 | tf_op jit(solution)/shard_map/while/body/jit(dynamic_update_index_in_dim)/dynamic_update_slice | solution.py:75
  406.3 1.9 fusion.56
  408.2 3.3 constant_dynamic-slice_fusion.5
  411.5 15.4 %fusion.57 = f32[128,16,128]{2,1,0:T(8,128)S(1)} fusion(f32[128,128,16]{0,2,1:T(8,128)S(1)} %bitcast.86, f32[128,128,128]{2,1,0:T(8,128)} %get-tuple-element.468), kind=kOutput, calls=%fused_computation.59.clone.1 | convolution fusion | flops 402653184 | bytes 10485760 | tf_op jit(solution)/shard_map/while/body/eval_jaxpr/gij,jgc->igc/dot_general | solution.py:70
  426.9 2.4 convolution_add_fusion.2
  429.3 26.6 %dynamic_update_slice.8 = f32[4,128,128,16]{1,0,3,2:T(4,128)} dynamic-update-slice(f32[4,128,128,16]{1,0,3,2:T(4,128)} %get-tuple-element.453, f32[1,128,128,16]{1,0,3,2:T(1,128)} %bitcast.88, s32[]{:T(128)} %get-tuple-element.451, s32[]{:T(128)} %constant.52.clone.1..sunk.1, s32[]{:T(128)} %constant.52.clone.1..sunk.1, s32[]{:T(128)} %constant.52.clone.1..sunk.1) | dynamic-update-slice | bytes 2097156 | tf_op jit(solution)/shard_map/while/body/jit(dynamic_update_index_in_dim)/dynamic_update_slice | solution.py:75
  455.9 1.9 fusion.56
  457.8 3.3 constant_dynamic-slice_fusion.5
  461.1 15.4 %fusion.57 = f32[128,16,128]{2,1,0:T(8,128)S(1)} fusion(f32[128,128,16]{0,2,1:T(8,128)S(1)} %bitcast.86, f32[128,128,128]{2,1,0:T(8,128)} %get-tuple-element.468), kind=kOutput, calls=%fused_computation.59.clone.1 | convolution fusion | flops 402653184 | bytes 10485760 | tf_op jit(solution)/shard_map/while/body/eval_jaxpr/gij,jgc->igc/dot_general | solution.py:70
  476.5 2.4 convolution_add_fusion.2
  478.9 26.6 %dynamic_update_slice.8 = f32[4,128,128,16]{1,0,3,2:T(4,128)} dynamic-update-slice(f32[4,128,128,16]{1,0,3,2:T(4,128)} %get-tuple-element.453, f32[1,128,128,16]{1,0,3,2:T(1,128)} %bitcast.88, s32[]{:T(128)} %get-tuple-element.451, s32[]{:T(128)} %constant.52.clone.1..sunk.1, s32[]{:T(128)} %constant.52.clone.1..sunk.1, s32[]{:T(128)} %constant.52.clone.1..sunk.1) | dynamic-update-slice | bytes 2097156 | tf_op jit(solution)/shard_map/while/body/jit(dynamic_update_index_in_dim)/dynamic_update_slice | solution.py:75
  505.5 1.9 fusion.56
  507.4 3.3 constant_dynamic-slice_fusion.5
  510.7 15.4 %fusion.57 = f32[128,16,128]{2,1,0:T(8,128)S(1)} fusion(f32[128,128,16]{0,2,1:T(8,128)S(1)} %bitcast.86, f32[128,128,128]{2,1,0:T(8,128)} %get-tuple-element.468), kind=kOutput, calls=%fused_computation.59.clone.1 | convolution fusion | flops 402653184 | bytes 10485760 | tf_op jit(solution)/shard_map/while/body/eval_jaxpr/gij,jgc->igc/dot_general | solution.py:70
  526.1 2.4 convolution_add_fusion.2
  528.5 26.6 %dynamic_update_slice.8 = f32[4,128,128,16]{1,0,3,2:T(4,128)} dynamic-update-slice(f32[4,128,128,16]{1,0,3,2:T(4,128)} %get-tuple-element.453, f32[1,128,128,16]{1,0,3,2:T(1,128)} %bitcast.88, s32[]{:T(128)} %get-tuple-element.451, s32[]{:T(128)} %constant.52.clone.1..sunk.1, s32[]{:T(128)} %constant.52.clone.1..sunk.1, s32[]{:T(128)} %constant.52.clone.1..sunk.1) | dynamic-update-slice | bytes 2097156 | tf_op jit(solution)/shard_map/while/body/jit(dynamic_update_index_in_dim)/dynamic_update_slice | solution.py:75
  555.1 1.9 fusion.56
  557.0 1.1 copy.54
  558.2 23.8 %all-gather.1 = f32[2048,16]{1,0:T(8,128)S(1)} all-gather(f32[128,16]{1,0:T(8,128)S(1)} %get-tuple-element.342), channel_id=3, replica_groups=mesh['seq'=16,'tp'=2] {'seq'}, dimensions={0}, use_global_device_ids=true | all-gather | bytes 139264 | tf_op jit(solution)/shard_map/all_gather | solution.py:17
  582.3 5.7 reshape.75
  588.0 12.8 %all-gather.7.cloned.1.call-done = f32[2048,16,16]{0,2,1:T(8,128)} async-done(((f32[128,16,16]{0,2,1:T(8,128)}), f32[2048,16,16]{0,2,1:T(8,128)}) %all-gather.7.cloned.1.call-update) | async-done | bytes 2097168 | tf_op jit(solution)/shard_map/all_gather | solution.py:17
  600.8 2.0 copy.68
  602.8 3.9 while.29
  606.7 0.5 copy.58
  607.2 6.0 bitcast_add_fusion
  613.2 5.1 fusion.22
  618.3 14.0 %convolution_convert_fusion.1 = bf16[512,4096]{1,0:T(8,128)(2,1)} fusion(bf16[512,2048]{0,1:T(8,128)(2,1)S(1)} %fusion.22, bf16[2048,4096]{1,0:T(8,128)(2,1)} %param.17), kind=kOutput, calls=%fused_computation.32 | convolution fusion | flops 8592031744 | bytes 23068672 | tf_op jit(solution)/shard_map/dot_general | solution.py:94
  632.3 53.6 %reduce-scatter.2.cloned.1.call-done = bf16[512,2048]{1,0:T(8,128)(2,1)} async-done(((bf16[512,4096]{1,0:T(8,128)(2,1)}), bf16[512,2048]{1,0:T(8,128)(2,1)}) %reduce-scatter.2.cloned.1.call-update) | async-done | bytes 2097168 | tf_op jit(solution)/shard_map/reduce_scatter | solution.py:95
  (79 shorter events, 4.1 us)
Async XLA Ops:
  6.5 4.9 copy-start.2
  6.5 5.0 copy-start.4
  6.5 263.6 %all-gather.5.cloned.1.call-start = ((), (), s32[]{:S(2)}) async-start(), calls=%async_computation.1 | async-start | bytes 53477376 | tf_op jit(solution)/shard_map/all_gather | solution.py:40
  11.3 589.5 %all-gather.7.cloned.1.call-start = ((), (), s32[]{:S(2)}) async-start(), calls=%async_computation.3 | async-start | bytes 2228224 | tf_op jit(solution)/shard_map/all_gather | solution.py:17
  67.2 9.4 %copy-start.1 = (f32[3,3,2048]{2,1,0:T(4,128)S(1)}, f32[3,3,2048]{2,1,0:T(4,128)}, u32[]{:S(2)}) copy-start(f32[3,3,2048]{2,1,0:T(4,128)} %param.13) | copy-start | bytes 221188
  304.8 11.0 %collective-permute-start = (bf16[2,3,2048]{2,1,0:T(4,128)(2,1)S(1)}, bf16[2,3,2048]{2,1,0:T(4,128)(2,1)S(1)}, u32[]{:S(2)}, u32[]{:S(2)}) collective-permute-start(bf16[2,3,2048]{2,1,0:T(4,128)(2,1)S(1)} %slice.35), channel_id=1, source_target_pairs={{0,2},{2,4},{4,6},{6,8},{8,10},{10,12},{12,14},{14,16},{16,18},{18... | collective-permute-start | bytes 73736 | tf_op jit(solution)/shard_map/ppermute | solution.py:12
  345.9 4.5 copy-start
  558.1 127.8 %reduce-scatter.2.cloned.1.call-start = ((), (), s32[]{:S(2)}) async-start(), calls=%async_computation.2 | async-start | bytes 6291456 | tf_op jit(solution)/shard_map/reduce_scatter | solution.py:95
  607.2 6.0 copy-start.3
Sparse Core Ops, SparseCore 0:
  11.5 258.6 all-gather.4
  558.2 42.5 all-gather.6
  632.4 53.4 reduce-scatter.1
where the time goes:
time: 696 us; the launch traced here: 692 us
  waiting for transfers between devices  252 us (36%)
  local copies, waits for them, and re-layouts  220 us (32%)
  matrix products  132 us (19%)
  other arithmetic  47.8 us (7%)
  blocking collectives  23.8 us (3%)
  between operations  13.3 us (2%)
    all_gather x1, waiting for transfers between devices, shards(): piece = lax.all_gather(w_in, 'seq', axis=0, tiled=True)  185 us
    dynamic_update_slice x4, local copies, waits for them, and re-layouts, shards(): lax.scan(advance, jnp.zeros((groups, order, width), jnp.float32), blocks)  106 us
    gather x2, local copies, waits for them, and re-layouts, shards(): toeplitz = jnp.where(lag[None] >= 0, kernel[:, jnp.maximum(lag, 0)], 0.0)  64.1 us
    dot_general x4, matrix products, advance(): local = jnp.einsum('gij,jgc->igc', toeplitz, block, precision=highest)  61.5 us
    reduce_scatter x1, waiting for transfers between devices, shards(): lax.psum_scatter(partial_value.astype(jnp.bfloat16), 'tp', scatter_dimens...  53.6 us
    dot_general x1, matrix products, shards(): jnp.dot(tokens, piece.reshape(piece.shape[0], 3 * chans), preferred_eleme...  33.7 us
    all_gather x1, blocking collectives, prefix(): everything = jax.tree.map(lambda part: lax.all_gather(part, axis), value)  23.8 us
    add x1, other arithmetic, shards(): filtered + short_taps[tap] * padded[taps - 1 - tap:taps - 1 - tap + count]  17.5 us
  transfers between devices with their start and end apart: 4, of which 3 were waited for; matrix products, arithmetic and copies ran while one was open for 13% of the time, Pallas kernels for 0%

commit v1 on v0

--- a/solution.py
+++ b/solution.py
@@ -4,6 +4,22 @@
 from jax.sharding import PartitionSpec as P
 
 SUB = 128
+
+
+def end_the_floor(vec, row_dim):
+    n_parts = jax.lax.psum(1, axis_name="seq")
+    q_next = vec
+    finding = sorted(((j, (j + 1) % n_parts) for j in range(n_parts)))
+    vals = [q_next]
+    tick = 1
+    while tick < n_parts:
+        q_next = jax.lax.ppermute(q_next, axis_name="seq", perm=finding)
+        vals.insert(0, q_next)
+        tick = tick + 1
+    all_values = jnp.concatenate(vals, axis=row_dim)
+    clean = jax.lax.axis_index("seq")
+    o_now = jnp.roll(all_values, (clean + 1) * vec.shape[row_dim], axis=row_dim)
+    return o_now
 
 
 def passed_along(block, axis, distance):
@@ -37,7 +53,7 @@
     width = chans // groups
     taps = short_taps.shape[0]
     highest = lax.Precision.HIGHEST
-    piece = lax.all_gather(w_in, "seq", axis=0, tiled=True)
+    piece = end_the_floor(w_in, 0)
     summed = jnp.dot(
         tokens, piece.reshape(piece.shape[0], 3 * chans), preferred_element_type=jnp.float32
     )

time: 696 us -> 1200 us (1.72)
  waiting for transfers between devices: 252 us -> 621 us
  local copies, waits for them, and re-layouts: 220 us -> 343 us
    ppermute x0 -> x15, waiting for transfers between devices: none -> 552 us  [end_the_floor(): q_next = jax.lax.ppermute(q_next, axis_name='seq', perm=finding)]
    all_gather x1 -> x0, waiting for transfers between devices: 185 us -> none  [shards(): piece = lax.all_gather(w_in, 'seq', axis=0, tiled=True)]
    unnamed x15 -> x108, local copies, waits for them, and re-layouts: 11.8 us -> 108 us
    dynamic_slice x0 -> x1, local copies, waits for them, and re-layouts: none -> 33.7 us  [end_the_floor(): o_now = jnp.roll(all_values, (clean + 1) * vec.shape[row_dim], axis=row_dim)]
  transfers between devices with their start and end apart: 4 -> 18, of which waited for: 3 -> 17; matrix products, arithmetic and copies ran while one was open for 13% -> 7% of each run, Pallas kernels for 0% -> 0%
where the time goes in v1:
time: 1200 us; the launch traced here: 1190 us
  waiting for transfers between devices  621 us (52%)
  local copies, waits for them, and re-layouts  343 us (29%)
  matrix products  132 us (11%)
  other arithmetic  49.8 us (4%)
  blocking collectives  26 us (2%)
  between operations  14.2 us (1%)
    ppermute x15, waiting for transfers between devices, end_the_floor(): q_next = jax.lax.ppermute(q_next, axis_name='seq', perm=finding)  552 us
    unnamed x108, local copies, waits for them, and re-layouts  108 us
    dynamic_update_slice x4, local copies, waits for them, and re-layouts, shards(): lax.scan(advance, jnp.zeros((groups, order, width), jnp.float32), blocks)  106 us
    gather x2, local copies, waits for them, and re-layouts, shards(): toeplitz = jnp.where(lag[None] >= 0, kernel[:, jnp.maximum(lag, 0)], 0.0)  63.9 us
    dot_general x4, matrix products, advance(): local = jnp.einsum('gij,jgc->igc', toeplitz, block, precision=highest)  61.5 us
    reduce_scatter x1, waiting for transfers between devices, shards(): lax.psum_scatter(partial_value.astype(jnp.bfloat16), 'tp', scatter_dimens...  53.6 us
    dynamic_slice x1, local copies, waits for them, and re-layouts, end_the_floor(): o_now = jnp.roll(all_values, (clean + 1) * vec.shape[row_dim], axis=row_dim)  33.7 us
    dot_general x1, matrix products, shards(): jnp.dot(tokens, piece.reshape(piece.shape[0], 3 * chans), preferred_eleme...  32.9 us
  transfers between devices with their start and end apart: 18, of which 17 were waited for; matrix products, arithmetic and copies ran while one was open for 7% of the time, Pallas kernels for 0%

profile of v1, /device:TPU:0, one launch (start us, length us, event | category | flops | bytes accessed | tf_op | source)
XLA Modules:
  0.0 1189.0 jit_solution(16856317648095894136)
XLA Ops:
  10.3 39.9 %collective-permute-done = bf16[256,3,2048]{0,2,1:T(8,128)(2,1)S(1)} collective-permute-done((bf16[256,3,2048]{0,2,1:T(8,128)(2,1)S(1)}, bf16[256,3,2048]{0,2,1:T(8,128)(2,1)S(1)}, u32[]{:S(2)}, u32[]{:S(2)}) %collective-permute-start) | collective-permute-done | bytes 3145760 | tf_op jit(solution)/shard_map/ppermute | solution.py:16
  51.8 39.4 %collective-permute-done.1 = bf16[256,3,2048]{0,2,1:T(8,128)(2,1)S(1)} collective-permute-done((bf16[256,3,2048]{0,2,1:T(8,128)(2,1)S(1)}, bf16[256,3,2048]{0,2,1:T(8,128)(2,1)S(1)}, u32[]{:S(2)}, u32[]{:S(2)}) %collective-permute-start.1) | collective-permute-done | bytes 3145760 | tf_op jit(solution)/shard_map/ppermute | solution.py:16
  92.8 39.4 %collective-permute-done.2 = bf16[256,3,2048]{0,2,1:T(8,128)(2,1)S(1)} collective-permute-done((bf16[256,3,2048]{0,2,1:T(8,128)(2,1)S(1)}, bf16[256,3,2048]{0,2,1:T(8,128)(2,1)S(1)}, u32[]{:S(2)}, u32[]{:S(2)}) %collective-permute-start.2) | collective-permute-done | bytes 3145760 | tf_op jit(solution)/shard_map/ppermute | solution.py:16
  133.8 39.4 %collective-permute-done.3 = bf16[256,3,2048]{0,2,1:T(8,128)(2,1)S(1)} collective-permute-done((bf16[256,3,2048]{0,2,1:T(8,128)(2,1)S(1)}, bf16[256,3,2048]{0,2,1:T(8,128)(2,1)S(1)}, u32[]{:S(2)}, u32[]{:S(2)}) %collective-permute-start.3) | collective-permute-done | bytes 3145760 | tf_op jit(solution)/shard_map/ppermute | solution.py:16
  174.9 39.4 %collective-permute-done.4 = bf16[256,3,2048]{0,2,1:T(8,128)(2,1)S(1)} collective-permute-done((bf16[256,3,2048]{0,2,1:T(8,128)(2,1)S(1)}, bf16[256,3,2048]{0,2,1:T(8,128)(2,1)S(1)}, u32[]{:S(2)}, u32[]{:S(2)}) %collective-permute-start.4) | collective-permute-done | bytes 3145760 | tf_op jit(solution)/shard_map/ppermute | solution.py:16
  215.9 39.4 %collective-permute-done.5 = bf16[256,3,2048]{0,2,1:T(8,128)(2,1)S(1)} collective-permute-done((bf16[256,3,2048]{0,2,1:T(8,128)(2,1)S(1)}, bf16[256,3,2048]{0,2,1:T(8,128)(2,1)S(1)}, u32[]{:S(2)}, u32[]{:S(2)}) %collective-permute-start.5) | collective-permute-done | bytes 3145760 | tf_op jit(solution)/shard_map/ppermute | solution.py:16
  257.0 39.4 %collective-permute-done.6 = bf16[256,3,2048]{0,2,1:T(8,128)(2,1)S(1)} collective-permute-done((bf16[256,3,2048]{0,2,1:T(8,128)(2,1)S(1)}, bf16[256,3,2048]{0,2,1:T(8,128)(2,1)S(1)}, u32[]{:S(2)}, u32[]{:S(2)}) %collective-permute-start.6) | collective-permute-done | bytes 3145760 | tf_op jit(solution)/shard_map/ppermute | solution.py:16
  298.0 39.4 %collective-permute-done.7 = bf16[256,3,2048]{0,2,1:T(8,128)(2,1)S(1)} collective-permute-done((bf16[256,3,2048]{0,2,1:T(8,128)(2,1)S(1)}, bf16[256,3,2048]{0,2,1:T(8,128)(2,1)S(1)}, u32[]{:S(2)}, u32[]{:S(2)}) %collective-permute-start.7) | collective-permute-done | bytes 3145760 | tf_op jit(solution)/shard_map/ppermute | solution.py:16
  339.1 39.4 %collective-permute-done.8 = bf16[256,3,2048]{0,2,1:T(8,128)(2,1)S(1)} collective-permute-done((bf16[256,3,2048]{0,2,1:T(8,128)(2,1)S(1)}, bf16[256,3,2048]{0,2,1:T(8,128)(2,1)S(1)}, u32[]{:S(2)}, u32[]{:S(2)}) %collective-permute-start.8) | collective-permute-done | bytes 3145760 | tf_op jit(solution)/shard_map/ppermute | solution.py:16
  380.1 39.4 %collective-permute-done.9 = bf16[256,3,2048]{0,2,1:T(8,128)(2,1)S(1)} collective-permute-done((bf16[256,3,2048]{0,2,1:T(8,128)(2,1)S(1)}, bf16[256,3,2048]{0,2,1:T(8,128)(2,1)S(1)}, u32[]{:S(2)}, u32[]{:S(2)}) %collective-permute-start.9) | collective-permute-done | bytes 3145760 | tf_op jit(solution)/shard_map/ppermute | solution.py:16
  421.3 39.4 %collective-permute-done.10 = bf16[256,3,2048]{0,2,1:T(8,128)(2,1)S(1)} collective-permute-done((bf16[256,3,2048]{0,2,1:T(8,128)(2,1)S(1)}, bf16[256,3,2048]{0,2,1:T(8,128)(2,1)S(1)}, u32[]{:S(2)}, u32[]{:S(2)}) %collective-permute-start.10) | collective-permute-done | bytes 3145760 | tf_op jit(solution)/shard_map/ppermute | solution.py:16
  462.4 39.4 %collective-permute-done.11 = bf16[256,3,2048]{0,2,1:T(8,128)(2,1)S(1)} collective-permute-done((bf16[256,3,2048]{0,2,1:T(8,128)(2,1)S(1)}, bf16[256,3,2048]{0,2,1:T(8,128)(2,1)S(1)}, u32[]{:S(2)}, u32[]{:S(2)}) %collective-permute-start.11) | collective-permute-done | bytes 3145760 | tf_op jit(solution)/shard_map/ppermute | solution.py:16
  503.4 39.4 %collective-permute-done.12 = bf16[256,3,2048]{0,2,1:T(8,128)(2,1)S(1)} collective-permute-done((bf16[256,3,2048]{0,2,1:T(8,128)(2,1)S(1)}, bf16[256,3,2048]{0,2,1:T(8,128)(2,1)S(1)}, u32[]{:S(2)}, u32[]{:S(2)}) %collective-permute-start.12) | collective-permute-done | bytes 3145760 | tf_op jit(solution)/shard_map/ppermute | solution.py:16
  544.4 39.5 %collective-permute-done.13 = bf16[256,3,2048]{0,2,1:T(8,128)(2,1)} collective-permute-done((bf16[256,3,2048]{0,2,1:T(8,128)(2,1)S(1)}, bf16[256,3,2048]{0,2,1:T(8,128)(2,1)}, u32[]{:S(2)}, u32[]{:S(2)}) %collective-permute-start.13) | collective-permute-done | bytes 3145760 | tf_op jit(solution)/shard_map/ppermute | solution.py:16
  587.6 54.5 %gather_fusion = f32[16384,128]{1,0:T(8,128)} fusion(f32[128,128]{0,1:T(8,128)S(1)} %copy.64, s32[16384]{0:T(1024)S(1)} %bitcast_clamp_fusion), kind=kCustom, calls=%fused_computation | custom fusion | bytes 16842752 | tf_op jit(solution)/shard_map/gather | solution.py:77
  642.1 9.4 copy.52
  651.6 8.6 select_bitcast_fusion
  660.2 4.0 constant_dynamic-update-slice_fusion.31
  664.1 4.0 constant_dynamic-update-slice_fusion.30
  695.0 3.8 constant_dynamic-update-slice_fusion.15
  698.8 3.9 constant_dynamic-update-slice_fusion.14
  702.7 3.9 constant_dynamic-update-slice_fusion.13
  706.6 3.8 constant_dynamic-update-slice_fusion.12
  734.1 33.7 %constant_dynamic-slice_fusion.2 = bf16[4096,3,2048]{0,2,1:T(8,128)(2,1)} fusion(bf16[8192,3,2048]{0,2,1:T(8,128)(2,1)} %constant_dynamic-update-slice_fusion, s32[]{:T(128)S(6)} %select_n.41), kind=kLoop, calls=%fused_computation.91 | loop fusion | bytes 100663296 | tf_op jit(solution)/shard_map/jit(_roll_dynamic)/dynamic_slice | solution.py:21
  767.8 32.9 %convolution_convert_fusion = bf16[6144,512]{1,0:T(8,128)(2,1)S(1)} fusion(bf16[4096,6144]{0,1:T(8,128)(2,1)} %bitcast.92, bf16[512,4096]{1,0:T(8,128)(2,1)} %param.11), kind=kOutput, calls=%fused_computation.29 | convolution fusion | flops 25772949504 | bytes 60817408 | tf_op jit(solution)/shard_map/dot_general | solution.py:57
  807.8 11.6 maximum_convert_fusion
  819.4 17.9 %fusion.19 = f32[512,3,2048]{0,2,1:T(8,128)S(1)} fusion(f32[514,3,2048]{0,2,1:T(8,128)} %maximum_convert_fusion, f32[3,2048]{1,0:T(4,128)S(1)} %get-tuple-element.340, f32[3,2048]{1,0:T(4,128)S(1)} %get-tuple-element.341, f32[3,2048]{1,0:T(4,128)S(1)} %get-tuple-element.339), kind=kLoop, calls=%fused_computation.25 | loop fusion | flops 15728640 | bytes 50405376 | tf_op jit(solution)/shard_map/add | solution.py:65
  837.4 4.6 copy-done
  845.0 5.2 mul.184
  850.2 198.5 %while.30 = (s32[]{:T(128)}, f32[128,16,16]{1,2,0:T(8,128)S(1)}, f32[4,128,128,16]{1,0,3,2:T(4,128)}, f32[128,16,1]{1,0,2:T(8,128)S(1)}, f32[4,128,128,16]{1,0,3...) while((s32[]{:T(128)}, f32[128,16,16]{1,2,0:T(8,128)S(1)}, ...), condition=%wide.region_1.2_spmd.clone.clone.clone, body=%wide.region_0.1_spmd.clone.clone.clone.sunk | while | flops 504496128 | bytes 18252936 | solution.py:91
  850.5 3.3 constant_dynamic-slice_fusion.6
  853.8 15.4 %fusion.57 = f32[128,16,128]{2,1,0:T(8,128)S(1)} fusion(f32[128,128,16]{0,2,1:T(8,128)S(1)} %bitcast.89, f32[128,128,128]{2,1,0:T(8,128)} %get-tuple-element.468), kind=kOutput, calls=%fused_computation.92.clone.1 | convolution fusion | flops 402653184 | bytes 10485760 | tf_op jit(solution)/shard_map/while/body/eval_jaxpr/gij,jgc->igc/dot_general | solution.py:86
  871.6 26.5 %dynamic_update_slice.8 = f32[4,128,128,16]{1,0,3,2:T(4,128)} dynamic-update-slice(f32[4,128,128,16]{1,0,3,2:T(4,128)} %get-tuple-element.453, f32[1,128,128,16]{1,0,3,2:T(1,128)} %bitcast.91, s32[]{:T(128)} %get-tuple-element.451, s32[]{:T(128)} %constant.77.clone.1..sunk.1, s32[]{:T(128)} %constant.77.clone.1..sunk.1, s32[]{:T(128)} %constant.77.clone.1..sunk.1) | dynamic-update-slice | bytes 2097156 | tf_op jit(solution)/shard_map/while/body/jit(dynamic_update_index_in_dim)/dynamic_update_slice | solution.py:91
  900.0 3.3 constant_dynamic-slice_fusion.6
  903.4 15.4 %fusion.57 = f32[128,16,128]{2,1,0:T(8,128)S(1)} fusion(f32[128,128,16]{0,2,1:T(8,128)S(1)} %bitcast.89, f32[128,128,128]{2,1,0:T(8,128)} %get-tuple-element.468), kind=kOutput, calls=%fused_computation.92.clone.1 | convolution fusion | flops 402653184 | bytes 10485760 | tf_op jit(solution)/shard_map/while/body/eval_jaxpr/gij,jgc->igc/dot_general | solution.py:86
  921.2 26.5 %dynamic_update_slice.8 = f32[4,128,128,16]{1,0,3,2:T(4,128)} dynamic-update-slice(f32[4,128,128,16]{1,0,3,2:T(4,128)} %get-tuple-element.453, f32[1,128,128,16]{1,0,3,2:T(1,128)} %bitcast.91, s32[]{:T(128)} %get-tuple-element.451, s32[]{:T(128)} %constant.77.clone.1..sunk.1, s32[]{:T(128)} %constant.77.clone.1..sunk.1, s32[]{:T(128)} %constant.77.clone.1..sunk.1) | dynamic-update-slice | bytes 2097156 | tf_op jit(solution)/shard_map/while/body/jit(dynamic_update_index_in_dim)/dynamic_update_slice | solution.py:91
  953.0 15.4 %fusion.57 = f32[128,16,128]{2,1,0:T(8,128)S(1)} fusion(f32[128,128,16]{0,2,1:T(8,128)S(1)} %bitcast.89, f32[128,128,128]{2,1,0:T(8,128)} %get-tuple-element.468), kind=kOutput, calls=%fused_computation.92.clone.1 | convolution fusion | flops 402653184 | bytes 10485760 | tf_op jit(solution)/shard_map/while/body/eval_jaxpr/gij,jgc->igc/dot_general | solution.py:86
  970.7 26.5 %dynamic_update_slice.8 = f32[4,128,128,16]{1,0,3,2:T(4,128)} dynamic-update-slice(f32[4,128,128,16]{1,0,3,2:T(4,128)} %get-tuple-element.453, f32[1,128,128,16]{1,0,3,2:T(1,128)} %bitcast.91, s32[]{:T(128)} %get-tuple-element.451, s32[]{:T(128)} %constant.77.clone.1..sunk.1, s32[]{:T(128)} %constant.77.clone.1..sunk.1, s32[]{:T(128)} %constant.77.clone.1..sunk.1) | dynamic-update-slice | bytes 2097156 | tf_op jit(solution)/shard_map/while/body/jit(dynamic_update_index_in_dim)/dynamic_update_slice | solution.py:91
  1002.5 15.4 %fusion.57 = f32[128,16,128]{2,1,0:T(8,128)S(1)} fusion(f32[128,128,16]{0,2,1:T(8,128)S(1)} %bitcast.89, f32[128,128,128]{2,1,0:T(8,128)} %get-tuple-element.468), kind=kOutput, calls=%fused_computation.92.clone.1 | convolution fusion | flops 402653184 | bytes 10485760 | tf_op jit(solution)/shard_map/while/body/eval_jaxpr/gij,jgc->igc/dot_general | solution.py:86
  1020.3 26.5 %dynamic_update_slice.8 = f32[4,128,128,16]{1,0,3,2:T(4,128)} dynamic-update-slice(f32[4,128,128,16]{1,0,3,2:T(4,128)} %get-tuple-element.453, f32[1,128,128,16]{1,0,3,2:T(1,128)} %bitcast.91, s32[]{:T(128)} %get-tuple-element.451, s32[]{:T(128)} %constant.77.clone.1..sunk.1, s32[]{:T(128)} %constant.77.clone.1..sunk.1, s32[]{:T(128)} %constant.77.clone.1..sunk.1) | dynamic-update-slice | bytes 2097156 | tf_op jit(solution)/shard_map/while/body/jit(dynamic_update_index_in_dim)/dynamic_update_slice | solution.py:91
  1050.0 26.0 %all-gather.1 = f32[2048,16]{1,0:T(8,128)S(1)} all-gather(f32[128,16]{1,0:T(8,128)S(1)} %copy-done.33), channel_id=3, replica_groups=mesh['seq'=16,'tp'=2] {'seq'}, dimensions={0}, use_global_device_ids=true | all-gather | bytes 139264 | tf_op jit(solution)/shard_map/all_gather | solution.py:33
  1076.3 5.7 reshape.75
  1082.1 14.6 %all-gather.4.cloned.1.call-done = f32[2048,16,16]{0,2,1:T(8,128)} async-done(((f32[128,16,16]{0,2,1:T(8,128)}), f32[2048,16,16]{0,2,1:T(8,128)}) %all-gather.4.cloned.1.call-update) | async-done | bytes 2097168 | tf_op jit(solution)/shard_map/all_gather | solution.py:33
  1098.6 3.9 while.29
  1103.0 6.0 bitcast_add_fusion
  1109.0 5.1 fusion.22
  1114.2 13.9 %convolution_convert_fusion.1 = bf16[512,4096]{1,0:T(8,128)(2,1)} fusion(bf16[512,2048]{0,1:T(8,128)(2,1)S(1)} %fusion.22, bf16[2048,4096]{1,0:T(8,128)(2,1)} %param.17), kind=kOutput, calls=%fused_computation.32 | convolution fusion | flops 8592031744 | bytes 23068672 | tf_op jit(solution)/shard_map/dot_general | solution.py:110
  1128.1 53.6 %reduce-scatter.2.cloned.1.call-done = bf16[512,2048]{1,0:T(8,128)(2,1)} async-done(((bf16[512,4096]{1,0:T(8,128)(2,1)}), bf16[512,2048]{1,0:T(8,128)(2,1)}) %reduce-scatter.2.cloned.1.call-update) | async-done | bytes 2097168 | tf_op jit(solution)/shard_map/reduce_scatter | solution.py:111
  (200 shorter events, 120.7 us)
Async XLA Ops:
  6.5 1090.1 %all-gather.4.cloned.1.call-start = ((), (), s32[]{:S(2)}) async-start(), calls=%async_computation.2 | async-start | bytes 2228224 | tf_op jit(solution)/shard_map/all_gather | solution.py:33
  9.7 40.5 %collective-permute-start = (bf16[256,3,2048]{0,2,1:T(8,128)(2,1)S(1)}, bf16[256,3,2048]{0,2,1:T(8,128)(2,1)S(1)}, u32[]{:S(2)}, u32[]{:S(2)}) collective-permute-start(bf16[256,3,2048]{0,2,1:T(8,128)(2,1)S(1)} %copy.46), channel_id=1, source_target_pairs={{0,2},{2,4},{4,6},{6,8},{8,10},{10,12},{12,14},{14,16},{16,18},{18... | collective-permute-start | bytes 9437192 | tf_op jit(solution)/shard_map/ppermute | solution.py:16
  50.2 1.6 copy-start.1
  51.8 39.4 %collective-permute-start.1 = (bf16[256,3,2048]{0,2,1:T(8,128)(2,1)S(1)}, bf16[256,3,2048]{0,2,1:T(8,128)(2,1)S(1)}, u32[]{:S(2)}, u32[]{:S(2)}) collective-permute-start(bf16[256,3,2048]{0,2,1:T(8,128)(2,1)S(1)} %collective-permute-done), channel_id=1, source_target_pairs={{0,2},{2,4},{4,6},{6,8},{8,10},{10,12},{12,14},{14,16},{16,18},{18... | collective-permute-start | bytes 9437192 | tf_op jit(solution)/shard_map/ppermute | solution.py:16
  92.8 39.4 %collective-permute-start.2 = (bf16[256,3,2048]{0,2,1:T(8,128)(2,1)S(1)}, bf16[256,3,2048]{0,2,1:T(8,128)(2,1)S(1)}, u32[]{:S(2)}, u32[]{:S(2)}) collective-permute-start(bf16[256,3,2048]{0,2,1:T(8,128)(2,1)S(1)} %collective-permute-done.1), channel_id=1, source_target_pairs={{0,2},{2,4},{4,6},{6,8},{8,10},{10,12},{12,14},{14,16},{16,18},{18... | collective-permute-start | bytes 9437192 | tf_op jit(solution)/shard_map/ppermute | solution.py:16
  133.8 39.4 %collective-permute-start.3 = (bf16[256,3,2048]{0,2,1:T(8,128)(2,1)S(1)}, bf16[256,3,2048]{0,2,1:T(8,128)(2,1)S(1)}, u32[]{:S(2)}, u32[]{:S(2)}) collective-permute-start(bf16[256,3,2048]{0,2,1:T(8,128)(2,1)S(1)} %collective-permute-done.2), channel_id=1, source_target_pairs={{0,2},{2,4},{4,6},{6,8},{8,10},{10,12},{12,14},{14,16},{16,18},{18... | collective-permute-start | bytes 9437192 | tf_op jit(solution)/shard_map/ppermute | solution.py:16
  173.2 1.7 copy-start.7
  174.9 39.4 %collective-permute-start.4 = (bf16[256,3,2048]{0,2,1:T(8,128)(2,1)S(1)}, bf16[256,3,2048]{0,2,1:T(8,128)(2,1)S(1)}, u32[]{:S(2)}, u32[]{:S(2)}) collective-permute-start(bf16[256,3,2048]{0,2,1:T(8,128)(2,1)S(1)} %collective-permute-done.3), channel_id=1, source_target_pairs={{0,2},{2,4},{4,6},{6,8},{8,10},{10,12},{12,14},{14,16},{16,18},{18... | collective-permute-start | bytes 9437192 | tf_op jit(solution)/shard_map/ppermute | solution.py:16
  215.9 39.4 %collective-permute-start.5 = (bf16[256,3,2048]{0,2,1:T(8,128)(2,1)S(1)}, bf16[256,3,2048]{0,2,1:T(8,128)(2,1)S(1)}, u32[]{:S(2)}, u32[]{:S(2)}) collective-permute-start(bf16[256,3,2048]{0,2,1:T(8,128)(2,1)S(1)} %collective-permute-done.4), channel_id=1, source_target_pairs={{0,2},{2,4},{4,6},{6,8},{8,10},{10,12},{12,14},{14,16},{16,18},{18... | collective-permute-start | bytes 9437192 | tf_op jit(solution)/shard_map/ppermute | solution.py:16
  255.3 1.7 copy-start.11
  257.0 39.4 %collective-permute-start.6 = (bf16[256,3,2048]{0,2,1:T(8,128)(2,1)S(1)}, bf16[256,3,2048]{0,2,1:T(8,128)(2,1)S(1)}, u32[]{:S(2)}, u32[]{:S(2)}) collective-permute-start(bf16[256,3,2048]{0,2,1:T(8,128)(2,1)S(1)} %collective-permute-done.5), channel_id=1, source_target_pairs={{0,2},{2,4},{4,6},{6,8},{8,10},{10,12},{12,14},{14,16},{16,18},{18... | collective-permute-start | bytes 9437192 | tf_op jit(solution)/shard_map/ppermute | solution.py:16
  296.3 1.6 copy-start.13
  298.0 39.4 %collective-permute-start.7 = (bf16[256,3,2048]{0,2,1:T(8,128)(2,1)S(1)}, bf16[256,3,2048]{0,2,1:T(8,128)(2,1)S(1)}, u32[]{:S(2)}, u32[]{:S(2)}) collective-permute-start(bf16[256,3,2048]{0,2,1:T(8,128)(2,1)S(1)} %collective-permute-done.6), channel_id=1, source_target_pairs={{0,2},{2,4},{4,6},{6,8},{8,10},{10,12},{12,14},{14,16},{16,18},{18... | collective-permute-start | bytes 9437192 | tf_op jit(solution)/shard_map/ppermute | solution.py:16
  337.4 1.7 copy-start.15
  339.1 39.4 %collective-permute-start.8 = (bf16[256,3,2048]{0,2,1:T(8,128)(2,1)S(1)}, bf16[256,3,2048]{0,2,1:T(8,128)(2,1)S(1)}, u32[]{:S(2)}, u32[]{:S(2)}) collective-permute-start(bf16[256,3,2048]{0,2,1:T(8,128)(2,1)S(1)} %collective-permute-done.7), channel_id=1, source_target_pairs={{0,2},{2,4},{4,6},{6,8},{8,10},{10,12},{12,14},{14,16},{16,18},{18... | collective-permute-start | bytes 9437192 | tf_op jit(solution)/shard_map/ppermute | solution.py:16
  378.4 1.7 copy-start.17
  380.1 39.4 %collective-permute-start.9 = (bf16[256,3,2048]{0,2,1:T(8,128)(2,1)S(1)}, bf16[256,3,2048]{0,2,1:T(8,128)(2,1)S(1)}, u32[]{:S(2)}, u32[]{:S(2)}) collective-permute-start(bf16[256,3,2048]{0,2,1:T(8,128)(2,1)S(1)} %collective-permute-done.8), channel_id=1, source_target_pairs={{0,2},{2,4},{4,6},{6,8},{8,10},{10,12},{12,14},{14,16},{16,18},{18... | collective-permute-start | bytes 9437192 | tf_op jit(solution)/shard_map/ppermute | solution.py:16
  419.5 1.8 copy-start.19
  421.3 39.4 %collective-permute-start.10 = (bf16[256,3,2048]{0,2,1:T(8,128)(2,1)S(1)}, bf16[256,3,2048]{0,2,1:T(8,128)(2,1)S(1)}, u32[]{:S(2)}, u32[]{:S(2)}) collective-permute-start(bf16[256,3,2048]{0,2,1:T(8,128)(2,1)S(1)} %collective-permute-done.9), channel_id=1, source_target_pairs={{0,2},{2,4},{4,6},{6,8},{8,10},{10,12},{12,14},{14,16},{16,18},{18... | collective-permute-start | bytes 9437192 | tf_op jit(solution)/shard_map/ppermute | solution.py:16
  460.6 1.7 copy-start.21
  462.4 39.4 %collective-permute-start.11 = (bf16[256,3,2048]{0,2,1:T(8,128)(2,1)S(1)}, bf16[256,3,2048]{0,2,1:T(8,128)(2,1)S(1)}, u32[]{:S(2)}, u32[]{:S(2)}) collective-permute-start(bf16[256,3,2048]{0,2,1:T(8,128)(2,1)S(1)} %collective-permute-done.10), channel_id=1, source_target_pairs={{0,2},{2,4},{4,6},{6,8},{8,10},{10,12},{12,14},{14,16},{16,18},{18... | collective-permute-start | bytes 9437192 | tf_op jit(solution)/shard_map/ppermute | solution.py:16
  503.4 39.4 %collective-permute-start.12 = (bf16[256,3,2048]{0,2,1:T(8,128)(2,1)S(1)}, bf16[256,3,2048]{0,2,1:T(8,128)(2,1)S(1)}, u32[]{:S(2)}, u32[]{:S(2)}) collective-permute-start(bf16[256,3,2048]{0,2,1:T(8,128)(2,1)S(1)} %collective-permute-done.11), channel_id=1, source_target_pairs={{0,2},{2,4},{4,6},{6,8},{8,10},{10,12},{12,14},{14,16},{16,18},{18... | collective-permute-start | bytes 9437192 | tf_op jit(solution)/shard_map/ppermute | solution.py:16
  542.8 1.6 copy-start.25
  544.4 39.5 %collective-permute-start.13 = (bf16[256,3,2048]{0,2,1:T(8,128)(2,1)S(1)}, bf16[256,3,2048]{0,2,1:T(8,128)(2,1)}, u32[]{:S(2)}, u32[]{:S(2)}) collective-permute-start(bf16[256,3,2048]{0,2,1:T(8,128)(2,1)S(1)} %collective-permute-done.12), channel_id=1, source_target_pairs={{0,2},{2,4},{4,6},{6,8},{8,10},{10,12},{12,14},{14,16},{16,18},{18... | collective-permute-start | bytes 9437192 | tf_op jit(solution)/shard_map/ppermute | solution.py:16
  583.9 76.2 %collective-permute-start.14 = (bf16[256,3,2048]{0,2,1:T(8,128)(2,1)}, bf16[256,3,2048]{0,2,1:T(8,128)(2,1)}, u32[]{:S(2)}, u32[]{:S(2)}) collective-permute-start(bf16[256,3,2048]{0,2,1:T(8,128)(2,1)} %collective-permute-done.13), channel_id=1, source_target_pairs={{0,2},{2,4},{4,6},{6,8},{8,10},{10,12},{12,14},{14,16},{16,18},{18... | collective-permute-start | bytes 9437192 | tf_op jit(solution)/shard_map/ppermute | solution.py:16
  642.1 9.4 copy-start.34
  651.6 16.5 %copy-start.26 = (bf16[256,3,2048]{0,2,1:T(8,128)(2,1)S(1)}, bf16[256,3,2048]{0,2,1:T(8,128)(2,1)}, u32[]{:S(2)}) copy-start(bf16[256,3,2048]{0,2,1:T(8,128)(2,1)} %copy-done.25) | copy-start | bytes 9437188
  660.2 9.9 copy-start.24
  660.2 11.8 copy-start.22
  664.1 9.7 copy-start.20
  668.1 7.6 copy-start.18
  670.0 7.6 copy-start.16
  671.9 7.6 copy-start.14
  673.8 7.7 copy-start.12
  675.7 7.7 copy-start.10
  677.6 7.7 copy-start.8
  679.6 7.7 copy-start.6
  681.5 7.7 copy-start.4
  683.4 7.7 copy-start.2
  800.8 2.6 copy-start.27
  804.6 2.1 collective-permute-start.15
  837.4 4.6 copy-start
  842.0 8.2 copy-start.29
  842.0 8.2 copy-start.31
  842.0 8.2 copy-start.32
  850.2 199.7 %copy-start.33 = (f32[128,16]{1,0:T(8,128)S(1)}, f32[128,16]{1,0:T(8,128)}, u32[]{:S(2)}) copy-start(f32[128,16]{1,0:T(8,128)} %get-tuple-element.342) | copy-start | bytes 24580
  1049.9 131.8 %reduce-scatter.2.cloned.1.call-start = ((), (), s32[]{:S(2)}) async-start(), calls=%async_computation.1 | async-start | bytes 6291456 | tf_op jit(solution)/shard_map/reduce_scatter | solution.py:111
  1076.3 32.7 %copy-start.35 = (f32[2048]{0:T(1024)S(1)}, f32[2048]{0:T(1024)}, u32[]{:S(2)}) copy-start(f32[2048]{0:T(1024)} %param.16) | copy-start | bytes 24580
  (6 other events, 7.8 us)
Sparse Core Ops, SparseCore 0:
  1050.0 46.5 all-gather.3
  1128.2 53.4 reduce-scatter.1
